TPU v7x, 128 devices: a whole 4x4x4 slice. The times are simulated.
128 devices in a mesh: cuts: 2 (over x_hi), section: 4 (over y), dp: 16 (over z, x_lo, core).
Axes of the slice: x: 4 (x_hi: 2, x_lo: 2; x = x_hi * 2 + x_lo), y: 4, z: 4, core: 2. Of those that a mesh axis runs over, the one named last changes fastest.
Arguments:
- activations: bfloat16 [2, 4, 4096, 4096], P('cuts', 'section', 'dp'), may hold values from -6 to 6
- upstream_grad: bfloat16 [2, 4, 4096, 4096], P('cuts', 'section', 'dp'), may hold values from -6 to 6
- routes: int32 [2, 4, 4096, 4], P('cuts', 'section', 'dp'), may hold values from 0 to 15, as said below
- router_probs: float32 [2, 4, 4096, 4], P('cuts', 'section', 'dp'), may hold values from 0.2 to 1
- gate_weight: bfloat16 [4, 5376, 4096], P('section', 'dp'), may hold values from -0.09375 to 0.09375
- up_weight: bfloat16 [4, 5376, 4096], P('section', 'dp'), may hold values from -0.09375 to 0.09375
- down_weight: bfloat16 [4, 5376, 4096], P('section', 'dp'), may hold values from -0.078125 to 0.078125
Outputs:
- grad_gate: bfloat16 [4, 5376, 4096], P('section', 'dp')
- grad_up: bfloat16 [4, 5376, 4096], P('section', 'dp')
- grad_down: bfloat16 [4, 5376, 4096], P('section', 'dp')
- prev_grad: bfloat16 [2, 4, 4096, 4096], P('cuts', 'section', 'dp')
Inputs may be any that keep to these rules, and one draw needn't show every extreme that they name: `routes`: each token names 4 different experts. In every aligned block of 256 tokens of one replica and section, from 32 to 64 tokens name expert 0, and in every draw some block has exactly 64.
All inputs are finite; a program needn't handle non-finite values.
Results may differ from a plain program's by a relative error of at most 0.025.
Values may be sent and summed in bfloat16 or wider, within the bound.
No kernel may reach another device: no remote copies, remote signals or barrier semaphores. Data moves between devices by JAX's collectives and lax.ppermute only.
A program may use at most 192 MiB of HBM per device.

v0:
```python
import jax
import jax.numpy as jnp
from jax import lax
from jax.sharding import PartitionSpec as P

CAP = 64


def from_behind(block, axis, distance):
    devices = range(lax.axis_size(axis))
    route = [(i - distance, i) for i in devices if i - distance in devices]
    return lax.ppermute(block, axis, route)


def contract_last(left, right):
    return lax.dot_general(
        left, right, (((1,), (1,)), ((), ())), preferred_element_type=jnp.float32
    )


def contract_first(left, right):
    return lax.dot_general(
        left, right, (((0,), (0,)), ((), ())), preferred_element_type=jnp.float32
    )


def per_device(
    activations, upstream_grad, routes, router_probs, gate_weight, up_weight, down_weight
):
    local_acts = activations[0, 0]
    local_grads = upstream_grad[0, 0]
    expert_hits = routes[0, 0] == 0
    router_weight = jnp.sum(jnp.where(expert_hits, router_probs[0, 0], jnp.float32(0.0)), axis=1)
    is_routed = jnp.any(expert_hits, axis=1)
    row_index = jnp.cumsum(is_routed.astype(jnp.int32)) - 1
    wanted = jnp.arange(CAP, dtype=jnp.int32)
    picker = ((row_index[None, :] == wanted[:, None]) & is_routed[None, :]).astype(jnp.bfloat16)
    scaled = (router_weight[:, None] * local_grads.astype(jnp.float32)).astype(jnp.bfloat16)
    packed_acts = jnp.dot(picker, local_acts, preferred_element_type=jnp.float32).astype(
        jnp.bfloat16
    )
    packed_grads = jnp.dot(picker, scaled, preferred_element_type=jnp.float32).astype(jnp.bfloat16)
    rows_acts, rows_grads = (
        lax.all_gather(packed_acts, "dp", axis=0, tiled=True),
        lax.all_gather(packed_grads, "dp", axis=0, tiled=True),
    )
    gate_local = gate_weight[0]
    up_local = up_weight[0]
    down_local = down_weight[0]
    gate_pre = contract_last(rows_acts, gate_local)
    up_pre = contract_last(rows_acts, up_local)
    sig_gate = jax.nn.sigmoid(gate_pre)
    silu_gate = gate_pre * sig_gate
    hidden = (silu_gate * up_pre).astype(jnp.bfloat16)
    hidden_grad = contract_last(rows_grads, down_local)
    gate_grad = (hidden_grad * up_pre * sig_gate * (1.0 + gate_pre * (1.0 - sig_gate))).astype(
        jnp.bfloat16
    )
    up_grad = (hidden_grad * silu_gate).astype(jnp.bfloat16)
    down_part = contract_first(hidden, rows_grads)
    gate_part = contract_first(gate_grad, rows_acts)
    up_part = contract_first(up_grad, rows_acts)
    gate_total, up_total, down_total = (
        lax.psum(gate_part.astype(jnp.bfloat16), "cuts").astype(jnp.float32),
        lax.psum(up_part.astype(jnp.bfloat16), "cuts").astype(jnp.float32),
        lax.psum(down_part.astype(jnp.bfloat16), "cuts").astype(jnp.float32),
    )
    input_rows = lax.psum_scatter(
        (
            jnp.dot(gate_grad, gate_local, preferred_element_type=jnp.float32)
            + jnp.dot(up_grad, up_local, preferred_element_type=jnp.float32)
        ).astype(jnp.bfloat16),
        "dp",
        scatter_dimension=0,
        tiled=True,
    )
    token_grad = contract_first(picker, input_rows).astype(jnp.bfloat16)
    prev_grad = from_behind(token_grad[None, None], "section", -1)
    grad_gate = gate_total.astype(jnp.bfloat16)[None]
    grad_up = up_total.astype(jnp.bfloat16)[None]
    grad_down = down_total.astype(jnp.bfloat16)[None]
    return (grad_gate, grad_up, grad_down, prev_grad)


def solution(mesh):
    placed = (
        P("cuts", "section", "dp", None),
        P("cuts", "section", "dp", None),
        P("cuts", "section", "dp", None),
        P("cuts", "section", "dp", None),
        P("section", "dp", None),
        P("section", "dp", None),
        P("section", "dp", None),
    )
    return jax.shard_map(
        per_device,
        mesh=mesh,
        in_specs=placed,
        out_specs=(
            P("section", "dp", None),
            P("section", "dp", None),
            P("section", "dp", None),
            P("cuts", "section", "dp", None),
        ),
        check_vma=False,
    )
```

profile of v0, /device:TPU:1, one launch (start us, length us, event | category | flops | bytes accessed | tf_op | source)
XLA Modules:
  0.0 471.8 jit_solution(16867495214857487981)
XLA Ops:
  7.2 0.9 select_reduce_fusion
  8.7 2.9 convolution_convert_fusion.4
  11.7 3.0 convolution_convert_fusion.5
  14.8 52.8 %all-gather.5.cloned.1.call-done = bf16[1024,4096]{1,0:T(8,128)(2,1)} async-done(((bf16[64,4096]{1,0:T(8,128)(2,1)}), bf16[1024,4096]{1,0:T(8,128)(2,1)}) %all-gather.5.cloned.1.call-update) | async-done | bytes 8388624 | tf_op jit(solution)/shard_map/all_gather | solution.py:44
  67.6 7.6 %fusion.7 = f32[1024,336]{0,1:T(8,128)} fusion(bf16[1024,4096]{1,0:T(8,128)(2,1)} %all-gather.5.cloned.1.call-done, bf16[1,336,4096]{2,1,0:T(8,128)(2,1)S(1)} %copy-done), kind=kOutput, calls=%fused_computation.15 | convolution fusion | flops 2818572288 | bytes 12517376 | tf_op jit(solution)/shard_map/dot_general | solution.py:16
  75.2 4.1 fusion.10
  79.3 43.7 %all-gather.3.cloned.1.call-done = bf16[1024,4096]{1,0:T(8,128)(2,1)} async-done(((bf16[64,4096]{1,0:T(8,128)(2,1)}), bf16[1024,4096]{1,0:T(8,128)(2,1)}) %all-gather.3.cloned.1.call-update) | async-done | bytes 8388624 | tf_op jit(solution)/shard_map/all_gather | solution.py:45
  123.0 8.3 %multiply_convert_fusion.1 = (bf16[1024,336]{0,1:T(8,128)(2,1)S(1)}, bf16[1024,336]{0,1:T(8,128)(2,1)S(1)}) fusion(f32[1024,336]{0,1:T(8,128)} %fusion.7, f32[1024,336]{0,1:T(8,128)} %fusion.10, bf16[1024,4096]{1,0:T(8,128)(2,1)} %all-gather.3.cloned.1.call-done, bf16[1,336,4096]{2,1,0:T(8,128)(2,1)} %param.13), kind=kOutput, calls=%fused_computation.26 | convolution fusion | flops 2823045120 | bytes 15269888 | tf_op jit(solution)/shard_map/dot_general | solution.py:16
  131.4 8.3 %fusion.5 = f32[1024,4096]{1,0:T(8,128)} fusion(bf16[1024,336]{0,1:T(8,128)(2,1)S(1)} %get-tuple-element.10, bf16[1,336,4096]{2,1,0:T(8,128)(2,1)S(1)} %copy-done), kind=kOutput, calls=%fused_computation.13 | convolution fusion | flops 2818572288 | bytes 20217856 | tf_op jit(solution)/shard_map/dot_general | solution.py:70
  139.7 10.2 %add_convert_fusion = bf16[1024,4096]{1,0:T(8,128)(2,1)} fusion(f32[1024,4096]{1,0:T(8,128)} %fusion.5, bf16[1024,336]{0,1:T(8,128)(2,1)S(1)} %get-tuple-element.9, bf16[1,336,4096]{2,1,0:T(8,128)(2,1)S(1)} %copy-done.5), kind=kOutput, calls=%fused_computation | convolution fusion | flops 2826960896 | bytes 28606464 | tf_op jit(solution)/shard_map/dot_general | solution.py:71
  150.0 7.8 %fusion.1 = bf16[1,336,4096]{2,1,0:T(8,128)(2,1)} fusion(bf16[1024,336]{0,1:T(8,128)(2,1)S(1)} %get-tuple-element.9, bf16[1024,4096]{1,0:T(8,128)(2,1)} %all-gather.5.cloned.1.call-done), kind=kOutput, calls=%fused_computation.6 | convolution fusion | flops 2819948544 | bytes 11829248 | tf_op jit(solution)/shard_map/dot_general | solution.py:22
  157.8 8.2 %fusion = bf16[1,336,4096]{2,1,0:T(8,128)(2,1)} fusion(bf16[1024,336]{0,1:T(8,128)(2,1)S(1)} %copy-done.9, bf16[1024,4096]{1,0:T(8,128)(2,1)} %all-gather.5.cloned.1.call-done), kind=kOutput, calls=%fused_computation.5 | convolution fusion | flops 2819948544 | bytes 11829248 | tf_op jit(solution)/shard_map/dot_general | solution.py:22
  166.1 4.5 fusion.2
  170.6 76.1 %reduce-scatter.2.cloned.1.call-done = bf16[64,4096]{1,0:T(8,128)(2,1)} async-done(((bf16[1024,4096]{1,0:T(8,128)(2,1)}), bf16[64,4096]{1,0:T(8,128)(2,1)}) %reduce-scatter.2.cloned.1.call-update) | async-done | bytes 524304 | tf_op jit(solution)/shard_map/reduce_scatter | solution.py:68
  246.7 1.8 fusion.3
  248.5 1.3 collective-permute-start
  249.8 45.3 %collective-permute-done = bf16[1,1,256,4096]{3,2,1,0:T(8,128)(2,1)S(1)} collective-permute-done((bf16[1,1,256,4096]{3,2,1,0:T(8,128)(2,1)S(1)}, bf16[1,1,256,4096]{3,2,1,0:T(8,128)(2,1)S(1)}, u32[]{:S(2)}, u32[]{:S(2)}) %collective-permute-start) | collective-permute-done | bytes 2097184 | tf_op jit(solution)/shard_map/ppermute | solution.py:12
  295.0 159.8 %all-reduce.3.cloned.1.call-done = (bf16[1,336,4096]{2,1,0:T(8,128)(2,1)}, bf16[1,336,4096]{2,1,0:T(8,128)(2,1)}, bf16[1,336,4096]{2,1,0:T(8,128)(2,1)}) async-done(((bf16[1,336,4096]{2,1,0:T(8,128)(2,1)}, bf16[1,336,4096]{2,1,0:T(8,128)(2,1)}, bf16[1,336,4096]{2,1,0:T(8,128)(2,1)}), (bf16[1,336,4096]{2,1,0:T(8,128)(2,1)}, bf16[1,336,4096]{2,1,0:T(8,128)(2,1)}, ...) | async-done | bytes 8257552 | tf_op jit(solution)/shard_map/psum | solution.py:64
  454.8 3.8 copy.15
  458.6 1.5 copy.16
  460.1 1.2 copy-done.2
  461.4 1.5 copy.17
  462.9 1.0 copy-done.7
  463.9 1.3 copy.18
  (44 shorter events, 0.9 us)
Async XLA Ops:
  7.2 60.4 %copy-start = (bf16[1,336,4096]{2,1,0:T(8,128)(2,1)S(1)}, bf16[1,336,4096]{2,1,0:T(8,128)(2,1)}, u32[]{:S(2)}) copy-start(bf16[1,336,4096]{2,1,0:T(8,128)(2,1)} %param.11) | copy-start | bytes 8257540
  7.2 60.4 %all-gather.5.cloned.1.call-start = ((), (), s32[]{:S(2)}) async-start(), calls=%async_computation.2 | async-start | bytes 8912896 | tf_op jit(solution)/shard_map/all_gather | solution.py:44
  11.6 111.4 %all-gather.3.cloned.1.call-start = ((), (), s32[]{:S(2)}) async-start(), calls=%async_computation.1 | async-start | bytes 8912896 | tf_op jit(solution)/shard_map/all_gather | solution.py:45
  14.7 232.0 %reduce-scatter.2.cloned.1.call-start = ((), (), s32[]{:S(2)}) async-start(), calls=%async_computation.3 | async-start | bytes 8912896 | tf_op jit(solution)/shard_map/reduce_scatter | solution.py:68
  67.6 7.7 %copy-start.4 = (bf16[1,336,4096]{2,1,0:T(8,128)(2,1)S(1)}, bf16[1,336,4096]{2,1,0:T(8,128)(2,1)}, u32[]{:S(2)}) copy-start(bf16[1,336,4096]{2,1,0:T(8,128)(2,1)} %param.12) | copy-start | bytes 8257540
  67.6 7.7 %copy-start.10 = (bf16[1024,4096]{1,0:T(8,128)(2,1)S(1)}, bf16[1024,4096]{1,0:T(8,128)(2,1)}, u32[]{:S(2)}) copy-start(bf16[1024,4096]{1,0:T(8,128)(2,1)} %all-gather.5.cloned.1.call-done) | copy-start | bytes 25165828
  131.4 8.3 %copy-start.8 = (bf16[1024,336]{0,1:T(8,128)(2,1)}, bf16[1024,336]{0,1:T(8,128)(2,1)S(1)}, u32[]{:S(2)}) copy-start(bf16[1024,336]{0,1:T(8,128)(2,1)S(1)} %get-tuple-element.10) | copy-start | bytes 2064388
  131.4 8.3 %copy-start.5 = (bf16[1,336,4096]{2,1,0:T(8,128)(2,1)S(1)}, bf16[1,336,4096]{2,1,0:T(8,128)(2,1)}, u32[]{:S(2)}) copy-start(bf16[1,336,4096]{2,1,0:T(8,128)(2,1)} %param.12) | copy-start | bytes 8257540
  149.9 7.9 %copy-start.9 = (bf16[1024,336]{0,1:T(8,128)(2,1)S(1)}, bf16[1024,336]{0,1:T(8,128)(2,1)}, u32[]{:S(2)}) copy-start(bf16[1024,336]{0,1:T(8,128)(2,1)} %copy-done.8) | copy-start | bytes 2064388
  149.9 304.9 %all-reduce.3.cloned.1.call-start = ((), (), s32[]{:S(2)}) async-start(), calls=%async_computation.4 | async-start | bytes 16515072 | tf_op jit(solution)/shard_map/psum | solution.py:64
  150.0 16.1 %slice-start = ((s8[8388608]{0:T(1024)(128)(4,1)}), s8[4194304]{0:T(1024)(128)(4,1)S(1)}, s32[]{:S(2)}) async-start(s8[8388608]{0:T(1024)(128)(4,1)} %bitcast.47), calls=%async_computation.5 | async-start | bytes 8388608
  157.8 8.3 %slice-start.1 = ((s8[8388608]{0:T(1024)(128)(4,1)}), s8[4194304]{0:T(1024)(128)(4,1)S(1)}, s32[]{:S(2)}) async-start(s8[8388608]{0:T(1024)(128)(4,1)} %bitcast.47), calls=%async_computation.6 | async-start | bytes 8388608
  157.8 8.3 %copy-start.11 = (f32[1024,336]{0,1:T(8,128)S(1)}, f32[1024,336]{0,1:T(8,128)}, u32[]{:S(2)}) copy-start(f32[1024,336]{0,1:T(8,128)} %fusion.7) | copy-start | bytes 4128772
  157.8 8.3 %copy-start.12 = (f32[1024,336]{0,1:T(8,128)S(1)}, f32[1024,336]{0,1:T(8,128)}, u32[]{:S(2)}) copy-start(f32[1024,336]{0,1:T(8,128)} %fusion.10) | copy-start | bytes 4128772
  248.5 46.6 %collective-permute-start = (bf16[1,1,256,4096]{3,2,1,0:T(8,128)(2,1)S(1)}, bf16[1,1,256,4096]{3,2,1,0:T(8,128)(2,1)S(1)}, u32[]{:S(2)}, u32[]{:S(2)}) collective-permute-start(bf16[1,1,256,4096]{3,2,1,0:T(8,128)(2,1)S(1)} %fusion.3), channel_id=1, source_target_pairs={{16,0},{32,16},{48,32},{17,1},{33,17},{49,33},{18,2},{34,18},{50,3... | collective-permute-start | bytes 6291464 | tf_op jit(solution)/shard_map/ppermute | solution.py:12
  295.0 159.8 %copy-start.6 = (bf16[1,1,256,4096]{3,2,1,0:T(8,128)(2,1)}, bf16[1,1,256,4096]{3,2,1,0:T(8,128)(2,1)S(1)}, u32[]{:S(2)}) copy-start(bf16[1,1,256,4096]{3,2,1,0:T(8,128)(2,1)S(1)} %collective-permute-done) | copy-start | bytes 6291460
  454.8 3.8 copy-start.3
  458.6 2.8 copy-start.2
  461.4 2.6 copy-start.7
  461.4 3.9 copy-start.1
Sparse Core Ops, SparseCore 0:
  11.8 55.7 all-gather.4
  69.9 53.1 all-gather.2
  150.0 96.6 reduce-scatter.1
  250.0 204.7 all-reduce.2
where the time goes:
time: 472 us
  waiting for transfers between devices  378 us (80%)
  matrix products  66.8 us (14%)
  between operations  13.9 us (3%)
  local copies, waits for them, and re-layouts  10.7 us (2%)
    psum x1, waiting for transfers between devices, per_device(): lax.psum(gate_part.astype(jnp.bfloat16), 'cuts').astype(jnp.float32)  160 us
    reduce_scatter x1, waiting for transfers between devices, per_device(): lax.psum_scatter((jnp.dot(gate_grad, gate_local, preferred_element_type=j...  76.1 us
    all_gather x1, waiting for transfers between devices, per_device(): lax.all_gather(packed_acts, 'dp', axis=0, tiled=True)  52.8 us
    ppermute x1, waiting for transfers between devices, from_behind(): return lax.ppermute(block, axis, route)  45.3 us
    all_gather x1, waiting for transfers between devices, per_device(): lax.all_gather(packed_grads, 'dp', axis=0, tiled=True)  43.7 us
    dot_general x4, matrix products, contract_first(): lax.dot_general(left, right, (((0,), (0,)), ((), ())), preferred_element_...  22.4 us
    dot_general x3, matrix products, contract_last(): lax.dot_general(left, right, (((1,), (1,)), ((), ())), preferred_element_...  20.1 us
    unnamed x34, local copies, waits for them, and re-layouts  10.5 us
  transfers between devices with their start and end apart: 5, of which 5 were waited for; matrix products, arithmetic and copies ran while one was open for 8% of the time, Pallas kernels for 0%

commit v1 on v0

--- a/solution.py
+++ b/solution.py
@@ -1,9 +1,25 @@
+import functools
 import jax
 import jax.numpy as jnp
 from jax import lax
 from jax.sharding import PartitionSpec as P
 
 CAP = 64
+
+
+def start_cards(x0, comm_axis):
+    return jnp.concatenate(
+        jax.lax.all_to_all(
+            jnp.stack(jax.lax.axis_size(comm_axis) * [x0]),
+            concat_axis=0,
+            axis_name=comm_axis,
+            split_axis=0,
+        ),
+        0,
+    )
+
+
+guide_values = functools.partial(start_cards, comm_axis="dp")
 
 
 def from_behind(block, axis, distance):
@@ -42,7 +58,7 @@
     packed_grads = jnp.dot(picker, scaled, preferred_element_type=jnp.float32).astype(jnp.bfloat16)
     rows_acts, rows_grads = (
         lax.all_gather(packed_acts, "dp", axis=0, tiled=True),
-        lax.all_gather(packed_grads, "dp", axis=0, tiled=True),
+        guide_values(packed_grads),
     )
     gate_local = gate_weight[0]
     up_local = up_weight[0]

time: 472 us -> 531 us (1.12)
  waiting for transfers between devices: 378 us -> 421 us
  starting transfers between devices: 1.46 us -> 9.16 us
    all_gather x1, waiting for transfers between devices: 52.8 us -> 136 us  [per_device(): lax.all_gather(packed_acts, 'dp', axis=0, tiled=True)]
    all_gather x1 -> x0, waiting for transfers between devices: 43.7 us -> none  [per_device(): lax.all_gather(packed_grads, 'dp', axis=0, tiled=True)]
    all_to_all x0 -> x1, starting transfers between devices: none -> 7.76 us  [start_cards(): jax.lax.all_to_all(jnp.stack(jax.lax.axis_size(comm_axis) * [x0]), concat...]
  transfers between devices with their start and end apart: 5 -> 5, of which waited for: 5 -> 4; matrix products, arithmetic and copies ran while one was open for 8% -> 8% of each run, Pallas kernels for 0% -> 0%
where the time goes in v1:
time: 531 us; the launch traced here: 530 us
  waiting for transfers between devices  421 us (79%)
  matrix products  69.4 us (13%)
  local copies, waits for them, and re-layouts  15 us (3%)
  between operations  13.8 us (3%)
  starting transfers between devices  9.16 us (2%)
    psum x1, waiting for transfers between devices, per_device(): lax.psum(gate_part.astype(jnp.bfloat16), 'cuts').astype(jnp.float32)  160 us
    all_gather x1, waiting for transfers between devices, per_device(): lax.all_gather(packed_acts, 'dp', axis=0, tiled=True)  136 us
    reduce_scatter x1, waiting for transfers between devices, per_device(): lax.psum_scatter((jnp.dot(gate_grad, gate_local, preferred_element_type=j...  80 us
    ppermute x1, waiting for transfers between devices, from_behind(): return lax.ppermute(block, axis, route)  45.2 us
    dot_general x4, matrix products, contract_first(): lax.dot_general(left, right, (((0,), (0,)), ((), ())), preferred_element_...  25.6 us
    dot_general x3, matrix products, contract_last(): lax.dot_general(left, right, (((1,), (1,)), ((), ())), preferred_element_...  20.1 us
  transfers between devices with their start and end apart: 5, of which 4 were waited for; matrix products, arithmetic and copies ran while one was open for 8% of the time, Pallas kernels for 0%

profile of v1, /device:TPU:1, one launch (start us, length us, event | category | flops | bytes accessed | tf_op | source)
XLA Modules:
  0.0 530.1 jit_solution(6373671663273915872)
XLA Ops:
  8.7 2.9 convolution_convert_fusion.4
  11.6 2.2 convolution_convert_fusion.5
  13.8 4.3 stack.2
  18.1 7.8 %all-to-all-start = ((bf16[16,64,4096]{2,1,0:T(8,128)(2,1)}), bf16[16,64,4096]{2,1,0:T(8,128)(2,1)}, u32[]{:S(2)}, u32[]{:S(2)}) async-start(bf16[16,64,4096]{2,1,0:T(8,128)(2,1)} %stack.2), calls=%async_computation | async-start | bytes 16777216 | tf_op jit(solution)/shard_map/all_to_all | solution.py:12
  25.9 136.2 %all-gather.2.cloned.1.call-done = bf16[1024,4096]{1,0:T(8,128)(2,1)} async-done(((bf16[64,4096]{1,0:T(8,128)(2,1)}), bf16[1024,4096]{1,0:T(8,128)(2,1)}) %all-gather.2.cloned.1.call-update) | async-done | bytes 8388624 | tf_op jit(solution)/shard_map/all_gather | solution.py:60
  162.1 7.6 %fusion.7 = f32[1024,336]{0,1:T(8,128)} fusion(bf16[1024,4096]{1,0:T(8,128)(2,1)} %all-gather.2.cloned.1.call-done, bf16[1,336,4096]{2,1,0:T(8,128)(2,1)S(1)} %copy-done), kind=kOutput, calls=%fused_computation.15 | convolution fusion | flops 2818572288 | bytes 12517376 | tf_op jit(solution)/shard_map/dot_general | solution.py:32
  169.7 4.1 fusion.10
  173.9 8.3 %multiply_convert_fusion.1 = (bf16[1024,336]{0,1:T(8,128)(2,1)S(1)}, bf16[1024,336]{0,1:T(8,128)(2,1)S(1)}) fusion(f32[1024,336]{0,1:T(8,128)} %fusion.7, f32[1024,336]{0,1:T(8,128)} %fusion.10, bf16[1024,4096]{1,0:T(8,128)(2,1)} %bitcast.3, bf16[1,336,4096]{2,1,0:T(8,128)(2,1)} %param.13), kind=kOutput, calls=%fused_computation.26 | convolution fusion | flops 2823045120 | bytes 15269888 | tf_op jit(solution)/shard_map/dot_general | solution.py:32
  182.2 8.4 %fusion.5 = f32[1024,4096]{1,0:T(8,128)} fusion(bf16[1024,336]{0,1:T(8,128)(2,1)S(1)} %get-tuple-element.10, bf16[1,336,4096]{2,1,0:T(8,128)(2,1)S(1)} %copy-done), kind=kOutput, calls=%fused_computation.13 | convolution fusion | flops 2818572288 | bytes 20217856 | tf_op jit(solution)/shard_map/dot_general | solution.py:86
  190.6 10.3 %add_convert_fusion = bf16[1024,4096]{1,0:T(8,128)(2,1)} fusion(f32[1024,4096]{1,0:T(8,128)} %fusion.5, bf16[1024,336]{0,1:T(8,128)(2,1)S(1)} %get-tuple-element.9, bf16[1,336,4096]{2,1,0:T(8,128)(2,1)S(1)} %copy-done.5), kind=kOutput, calls=%fused_computation | convolution fusion | flops 2826960896 | bytes 28606464 | tf_op jit(solution)/shard_map/dot_general | solution.py:87
  201.0 7.7 %fusion.1 = bf16[1,336,4096]{2,1,0:T(8,128)(2,1)} fusion(bf16[1024,336]{0,1:T(8,128)(2,1)S(1)} %get-tuple-element.9, bf16[1024,4096]{1,0:T(8,128)(2,1)} %all-gather.2.cloned.1.call-done), kind=kOutput, calls=%fused_computation.6 | convolution fusion | flops 2819948544 | bytes 11829248 | tf_op jit(solution)/shard_map/dot_general | solution.py:38
  208.7 7.8 %fusion = bf16[1,336,4096]{2,1,0:T(8,128)(2,1)} fusion(bf16[1024,336]{0,1:T(8,128)(2,1)S(1)} %copy-done.9, bf16[1024,4096]{1,0:T(8,128)(2,1)} %all-gather.2.cloned.1.call-done), kind=kOutput, calls=%fused_computation.5 | convolution fusion | flops 2819948544 | bytes 11829248 | tf_op jit(solution)/shard_map/dot_general | solution.py:38
  216.6 8.2 %fusion.2 = bf16[1,336,4096]{2,1,0:T(8,128)(2,1)} fusion(bf16[1024,4096]{1,0:T(8,128)(2,1)} %bitcast.3, f32[1024,336]{0,1:T(8,128)S(1)} %copy-done.12, f32[1024,336]{0,1:T(8,128)S(1)} %copy-done.11), kind=kOutput, calls=%fused_computation.7 | convolution fusion | flops 2822012928 | bytes 13893632 | tf_op jit(solution)/shard_map/dot_general | solution.py:38
  224.8 80.0 %reduce-scatter.2.cloned.1.call-done = bf16[64,4096]{1,0:T(8,128)(2,1)} async-done(((bf16[1024,4096]{1,0:T(8,128)(2,1)}), bf16[64,4096]{1,0:T(8,128)(2,1)}) %reduce-scatter.2.cloned.1.call-update) | async-done | bytes 524304 | tf_op jit(solution)/shard_map/reduce_scatter | solution.py:84
  304.9 1.8 fusion.3
  306.6 1.3 collective-permute-start
  307.9 45.2 %collective-permute-done = bf16[1,1,256,4096]{3,2,1,0:T(8,128)(2,1)S(1)} collective-permute-done((bf16[1,1,256,4096]{3,2,1,0:T(8,128)(2,1)S(1)}, bf16[1,1,256,4096]{3,2,1,0:T(8,128)(2,1)S(1)}, u32[]{:S(2)}, u32[]{:S(2)}) %collective-permute-start) | collective-permute-done | bytes 2097184 | tf_op jit(solution)/shard_map/ppermute | solution.py:28
  353.2 159.9 %all-reduce.3.cloned.1.call-done = (bf16[1,336,4096]{2,1,0:T(8,128)(2,1)}, bf16[1,336,4096]{2,1,0:T(8,128)(2,1)}, bf16[1,336,4096]{2,1,0:T(8,128)(2,1)}) async-done(((bf16[1,336,4096]{2,1,0:T(8,128)(2,1)}, bf16[1,336,4096]{2,1,0:T(8,128)(2,1)}, bf16[1,336,4096]{2,1,0:T(8,128)(2,1)}), (bf16[1,336,4096]{2,1,0:T(8,128)(2,1)}, bf16[1,336,4096]{2,1,0:T(8,128)(2,1)}, ...) | async-done | bytes 8257552 | tf_op jit(solution)/shard_map/psum | solution.py:80
  513.1 3.8 copy.15
  516.9 1.5 copy.16
  518.4 1.2 copy-done.2
  519.7 1.5 copy.17
  521.2 1.0 copy-done.7
  522.2 1.3 copy.18
  (39 shorter events, 1.7 us)
Async XLA Ops:
  7.2 154.9 %copy-start = (bf16[1,336,4096]{2,1,0:T(8,128)(2,1)S(1)}, bf16[1,336,4096]{2,1,0:T(8,128)(2,1)}, u32[]{:S(2)}) copy-start(bf16[1,336,4096]{2,1,0:T(8,128)(2,1)} %param.11) | copy-start | bytes 8257540
  7.2 154.9 %all-gather.2.cloned.1.call-start = ((), (), s32[]{:S(2)}) async-start(), calls=%async_computation.2 | async-start | bytes 8912896 | tf_op jit(solution)/shard_map/all_gather | solution.py:60
  18.1 155.7 %all-to-all-start = ((bf16[16,64,4096]{2,1,0:T(8,128)(2,1)}), bf16[16,64,4096]{2,1,0:T(8,128)(2,1)}, u32[]{:S(2)}, u32[]{:S(2)}) async-start(bf16[16,64,4096]{2,1,0:T(8,128)(2,1)} %stack.2), calls=%async_computation | async-start | bytes 16777216 | tf_op jit(solution)/shard_map/all_to_all | solution.py:12
  25.9 279.0 %reduce-scatter.2.cloned.1.call-start = ((), (), s32[]{:S(2)}) async-start(), calls=%async_computation.3 | async-start | bytes 8912896 | tf_op jit(solution)/shard_map/reduce_scatter | solution.py:84
  162.1 7.6 %copy-start.4 = (bf16[1,336,4096]{2,1,0:T(8,128)(2,1)S(1)}, bf16[1,336,4096]{2,1,0:T(8,128)(2,1)}, u32[]{:S(2)}) copy-start(bf16[1,336,4096]{2,1,0:T(8,128)(2,1)} %param.12) | copy-start | bytes 8257540
  162.1 7.6 %copy-start.10 = (bf16[1024,4096]{1,0:T(8,128)(2,1)S(1)}, bf16[1024,4096]{1,0:T(8,128)(2,1)}, u32[]{:S(2)}) copy-start(bf16[1024,4096]{1,0:T(8,128)(2,1)} %all-gather.2.cloned.1.call-done) | copy-start | bytes 25165828
  182.2 8.4 %copy-start.8 = (bf16[1024,336]{0,1:T(8,128)(2,1)}, bf16[1024,336]{0,1:T(8,128)(2,1)S(1)}, u32[]{:S(2)}) copy-start(bf16[1024,336]{0,1:T(8,128)(2,1)S(1)} %get-tuple-element.10) | copy-start | bytes 2064388
  182.2 8.4 %copy-start.5 = (bf16[1,336,4096]{2,1,0:T(8,128)(2,1)S(1)}, bf16[1,336,4096]{2,1,0:T(8,128)(2,1)}, u32[]{:S(2)}) copy-start(bf16[1,336,4096]{2,1,0:T(8,128)(2,1)} %param.12) | copy-start | bytes 8257540
  200.9 7.8 %copy-start.9 = (bf16[1024,336]{0,1:T(8,128)(2,1)S(1)}, bf16[1024,336]{0,1:T(8,128)(2,1)}, u32[]{:S(2)}) copy-start(bf16[1024,336]{0,1:T(8,128)(2,1)} %copy-done.8) | copy-start | bytes 2064388
  200.9 312.2 %all-reduce.3.cloned.1.call-start = ((), (), s32[]{:S(2)}) async-start(), calls=%async_computation.4 | async-start | bytes 16515072 | tf_op jit(solution)/shard_map/psum | solution.py:80
  208.7 7.8 %copy-start.11 = (f32[1024,336]{0,1:T(8,128)S(1)}, f32[1024,336]{0,1:T(8,128)}, u32[]{:S(2)}) copy-start(f32[1024,336]{0,1:T(8,128)} %fusion.7) | copy-start | bytes 4128772
  208.7 7.8 %copy-start.12 = (f32[1024,336]{0,1:T(8,128)S(1)}, f32[1024,336]{0,1:T(8,128)}, u32[]{:S(2)}) copy-start(f32[1024,336]{0,1:T(8,128)} %fusion.10) | copy-start | bytes 4128772
  306.6 46.5 %collective-permute-start = (bf16[1,1,256,4096]{3,2,1,0:T(8,128)(2,1)S(1)}, bf16[1,1,256,4096]{3,2,1,0:T(8,128)(2,1)S(1)}, u32[]{:S(2)}, u32[]{:S(2)}) collective-permute-start(bf16[1,1,256,4096]{3,2,1,0:T(8,128)(2,1)S(1)} %fusion.3), channel_id=1, source_target_pairs={{16,0},{32,16},{48,32},{17,1},{33,17},{49,33},{18,2},{34,18},{50,3... | collective-permute-start | bytes 6291464 | tf_op jit(solution)/shard_map/ppermute | solution.py:28
  353.2 159.9 %copy-start.6 = (bf16[1,1,256,4096]{3,2,1,0:T(8,128)(2,1)}, bf16[1,1,256,4096]{3,2,1,0:T(8,128)(2,1)S(1)}, u32[]{:S(2)}) copy-start(bf16[1,1,256,4096]{3,2,1,0:T(8,128)(2,1)S(1)} %collective-permute-done) | copy-start | bytes 6291460
  513.1 3.8 copy-start.3
  516.9 2.8 copy-start.2
  519.7 2.6 copy-start.7
  519.7 3.9 copy-start.1
Sparse Core Ops, SparseCore 0:
  11.8 150.2 all-gather.1
  201.1 103.7 reduce-scatter.1
  308.3 204.7 all-reduce.2
